TPU v7x, 256 devices: a whole 4x4x8 slice. The times are simulated.
256 devices in a mesh: seq: 32 (over z, y), head: 8 (over x, core).
Axes of the slice: x: 4, y: 4, z: 8, core: 2. Of those that a mesh axis runs over, the one named last changes fastest.
Arguments:
- hidden_states: bfloat16 [8, 5, 8192], P(None, None, 'seq'), may hold values from -6 to 6
- w_query: bfloat16 [8192, 8192], P('seq', 'head'), may hold values from -0.0625 to 0.0625
- w_key: bfloat16 [8192, 1024], P('seq', 'head'), may hold values from -0.15625 to 0.15625
- w_value: bfloat16 [8192, 1024], P('seq', 'head'), may hold values from -0.0625 to 0.0625
- w_out: bfloat16 [8192, 8192], P('head', 'seq'), may hold values from -0.0625 to 0.0625
- key_cache: bfloat16 [8, 32768, 1024], P(None, 'seq', 'head'), may hold values from -104 to 104
- value_cache: bfloat16 [8, 32768, 1024], P(None, 'seq', 'head'), may hold values from -6 to 6
- context_lengths: int32 [8], replicated, may hold values from 8192 to 32768, as said below
- keep_blocks: int32 [8, 256], P(None, 'seq'), may hold values from 0 to 1, as said below
Outputs:
- verify_out: bfloat16 [8, 5, 8192], P(None, None, 'seq')
- draft_out: bfloat16 [8, 4, 8192], P(None, None, 'seq')
Inputs may be any that keep to these rules, and one draw needn't show every extreme that they name: `keep_blocks`: block 0 of every sequence is kept. `context_lengths`: one sequence has length 32768.
All inputs are finite; a program needn't handle non-finite values.
Results may differ from a plain program's by a relative error of at most 0.017.
Values may be sent and summed in bfloat16 or wider, within the bound.
No kernel may reach another device: no remote copies, remote signals or barrier semaphores. Data moves between devices by JAX's collectives and lax.ppermute only.
A program may use at most 64 MiB of HBM per device.

v0:
```python
import jax
import jax.numpy as jnp
from jax import lax
from jax.sharding import PartitionSpec as P

HEAD_DIM = 128
BLOCK = 128
big_negative = -1e30


def rotate(values_in, positions):
    half_dim = HEAD_DIM // 2
    inverse = 500000.0 ** (-(jnp.arange(half_dim, dtype=jnp.float32) * 2.0) / HEAD_DIM)
    angles = positions[:, :, None, None].astype(jnp.float32) * inverse
    cosine = jnp.cos(angles)
    sine = jnp.sin(angles)
    first_half = values_in[..., :half_dim]
    second_half = values_in[..., half_dim:]
    return jnp.concatenate(
        [first_half * cosine - second_half * sine, second_half * cosine + first_half * sine],
        axis=-1,
    )


def partial_softmax(scores, mask_full, cache_values):
    masked = jnp.where(mask_full, scores, big_negative)
    peak_value = jnp.max(masked, axis=-1)
    weights = jnp.where(mask_full, jnp.exp(masked - peak_value[..., None]), 0.0)
    weighted = jnp.einsum(
        "bkjgt,btkd->bkjgd",
        weights.astype(jnp.bfloat16),
        cache_values,
        preferred_element_type=jnp.float32,
    )
    return (peak_value, jnp.sum(weights, axis=-1), weighted)


def finish(partials, new_scores, causal, new_values):
    peak_cache, total_sum, weighted = partials
    mask_full = causal[None, None, :, None, :]
    masked = jnp.where(mask_full, new_scores, big_negative)
    peak_value = jnp.maximum(peak_cache, jnp.max(masked, axis=-1))
    factor_old = jnp.exp(peak_cache - peak_value)
    weights = jnp.where(mask_full, jnp.exp(masked - peak_value[..., None]), 0.0)
    total_sum = total_sum * factor_old + jnp.sum(weights, axis=-1)
    weighted = weighted * factor_old[..., None] + jnp.einsum(
        "bkjgi,bikd->bkjgd",
        weights.astype(jnp.bfloat16),
        new_values,
        preferred_element_type=jnp.float32,
    )
    result = weighted / total_sum[..., None]
    batch_size, kv_local, positions_count, group_size, head_size = result.shape
    return result.transpose(0, 2, 1, 3, 4).reshape(
        batch_size * positions_count, kv_local * group_size * head_size
    )


def per_device(
    hidden_states,
    w_query,
    w_key,
    w_value,
    w_out,
    key_cache,
    value_cache,
    context_lengths,
    keep_blocks,
):
    seq_index = lax.axis_index("seq")
    batch_size, verify, width_local = hidden_states.shape
    draft_len = verify - 1
    kv_local = key_cache.shape[2] // HEAD_DIM
    heads_local = w_query.shape[1] // HEAD_DIM
    group_size = heads_local // kv_local
    ctx_local = key_cache.shape[1]
    score_scale = HEAD_DIM ** (-0.5)
    tok_rows = hidden_states.reshape(batch_size * verify, width_local)
    query_part = jnp.dot(tok_rows, w_query, preferred_element_type=jnp.float32)
    key_part = jnp.dot(tok_rows, w_key, preferred_element_type=jnp.float32)
    value_part = jnp.dot(tok_rows, w_value, preferred_element_type=jnp.float32)
    query_sum, key_sum, value_sum = lax.psum((query_part, key_part, value_part), "seq")
    positions = context_lengths[:, None] + jnp.arange(verify, dtype=jnp.int32)[None, :]
    query_rot = rotate(
        query_sum.reshape(batch_size, verify, heads_local, HEAD_DIM), positions
    ).astype(jnp.bfloat16)
    new_key = rotate(key_sum.reshape(batch_size, verify, kv_local, HEAD_DIM), positions).astype(
        jnp.bfloat16
    )
    new_values = value_sum.reshape(batch_size, verify, kv_local, HEAD_DIM).astype(jnp.bfloat16)
    grouped = query_rot.reshape(batch_size, verify, kv_local, group_size, HEAD_DIM)
    cache_keys = key_cache.reshape(batch_size, ctx_local, kv_local, HEAD_DIM)
    cache_values = value_cache.reshape(batch_size, ctx_local, kv_local, HEAD_DIM)
    scores = (
        jnp.einsum("bjkgd,btkd->bkjgt", grouped, cache_keys, preferred_element_type=jnp.float32)
        * score_scale
    )
    key_positions = seq_index * ctx_local + jnp.arange(ctx_local, dtype=jnp.int32)
    live_mask = key_positions[None, :] < context_lengths[:, None]
    kept_mask = live_mask & (jnp.repeat(keep_blocks, BLOCK, axis=1) > 0)
    target_peak, target_total, target_weighted = partial_softmax(
        scores, live_mask[:, None, None, None, :], cache_values
    )
    draft_peak, draft_total, draft_weighted = partial_softmax(
        scores[:, :, :draft_len], kept_mask[:, None, None, None, :], cache_values
    )
    peak_target, peak_draft = lax.pmax((target_peak, draft_peak), "seq")
    factor_target = jnp.exp(target_peak - peak_target)
    factor_draft = jnp.exp(draft_peak - peak_draft)
    sum_parts = lax.psum(
        (
            target_total * factor_target,
            target_weighted * factor_target[..., None],
            draft_total * factor_draft,
            draft_weighted * factor_draft[..., None],
        ),
        "seq",
    )
    merged = (peak_target, sum_parts[0], sum_parts[1], peak_draft, sum_parts[2], sum_parts[3])
    causal = jnp.arange(verify)[None, :] <= jnp.arange(verify)[:, None]
    new_scores = (
        jnp.einsum("bjkgd,bikd->bkjgi", grouped, new_key, preferred_element_type=jnp.float32)
        * score_scale
    )
    target_heads = finish(merged[0:3], new_scores, causal, new_values)
    draft_heads = finish(merged[3:6], new_scores[:, :, :draft_len], causal[:draft_len], new_values)
    attended = jnp.concatenate([target_heads, draft_heads], axis=0).astype(jnp.bfloat16)
    projected = jnp.dot(attended, w_out, preferred_element_type=jnp.float32)
    summed = lax.psum(projected.astype(jnp.bfloat16), "head")
    verify_out = summed[: batch_size * verify].reshape(batch_size, verify, summed.shape[1])
    draft_out = summed[batch_size * verify :].reshape(batch_size, draft_len, summed.shape[1])
    return (verify_out, draft_out)


def solution(mesh):
    placed = (
        P(None, None, "seq"),
        P("seq", "head"),
        P("seq", "head"),
        P("seq", "head"),
        P("head", "seq"),
        P(None, "seq", "head"),
        P(None, "seq", "head"),
        P(),
        P(None, "seq"),
    )
    return jax.shard_map(
        per_device,
        mesh=mesh,
        in_specs=placed,
        out_specs=(P(None, None, "seq"), P(None, None, "seq")),
        check_vma=False,
    )
```

profile of v0, /device:TPU:32, one launch (start us, length us, event | category | flops | bytes accessed | tf_op | source)
XLA Modules:
  0.0 634.3 jit_solution(9448252033808468446)
XLA Ops:
  7.3 0.9 copy.42
  8.2 1.2 convolution_bitcast_fusion
  9.4 0.7 copy.58
  10.6 0.6 reshape.256
  11.2 0.7 fusion.88
  11.9 0.6 slice.34
  12.8 144.7 %all-reduce.6.cloned.1.call-done = f32[8,5,8,128]{3,2,1,0:T(8,128)} async-done(((f32[8,5,8,128]{3,2,1,0:T(8,128)}), f32[8,5,8,128]{3,2,1,0:T(8,128)}) %all-reduce.6.cloned.1.call-update) | async-done | bytes 163856 | tf_op jit(solution)/shard_map/psum | solution.py:82
  157.5 1.1 subtract_convert_fusion
  158.7 0.9 select_reduce_fusion
  159.6 1.0 fusion.27
  160.9 1.0 fusion.30
  161.9 134.7 %all-reduce.2 = (f32[8,1,4,8]{3,2,0,1:T(4,128)}, f32[8,1,5,8]{3,2,0,1:T(8,128)S(1)}) all-reduce(f32[8,1,4,8]{3,2,0,1:T(4,128)} %bitcast.153, f32[8,1,5,8]{3,2,0,1:T(8,128)S(1)} %bitcast.151), channel_id=1, replica_groups=mesh['seq'=32,'head'=8] {'seq'}, use_global_device_ids=true, to_apply=%region_11.12 | all-reduce | flops 576 | bytes 4608 | tf_op jit(solution)/shard_map/pmax | solution.py:107
  296.6 1.4 bitcast_multiply_fusion
  298.0 1.4 bitcast_multiply_fusion.1
  299.4 138.9 %all-reduce = (f32[8,5,1,128]{3,1,0,2:T(8,128)}, f32[8,1,4,8]{3,2,0,1:T(4,128)}, bf16[40,128]{1,0:T(8,128)(2,1)}, f32[8,1,5,8]{3,2,0,1:T(8,128)}) all-reduce(f32[8,5,1,128]{3,1,0,2:T(8,128)} %reshape.256, f32[8,1,4,8]{3,2,0,1:T(4,128)} %get-tuple-element.35, f32[40,128]{1,0:T(8,128)} %fusion.88, ...), channel_id=1, replica_groups=mesh['seq'=32,'head'=8] {'seq'}, use_global_device_ids=true, to_apply=%region_4.5 | all-reduce | flops 10816 | bytes 76288 | tf_op jit(solution)/shard_map/psum | solution.py:82
  438.2 1.0 fusion.73
  439.3 1.4 fusion.66
  440.6 0.8 select_reduce_fusion.1
  442.0 2.0 fusion.47
  444.0 3.0 fusion.12
  447.1 1.2 fusion.20
  448.3 0.8 fusion.49
  449.1 0.7 fusion.75
  449.8 0.8 fusion.51
  450.6 0.8 fusion.78
  451.5 0.8 fusion.74
  452.3 147.3 %all-reduce.8.cloned.1.call-done = (f32[8,1,4,8,128]{4,3,2,0,1:T(8,128)}, f32[8,1,5,8,128]{4,3,2,0,1:T(8,128)}) async-done(((f32[8,1,4,8,128]{4,3,2,0,1:T(8,128)}, f32[8,1,5,8,128]{4,3,2,0,1:T(8,128)}), (f32[8,1,4,8,128]{4,3,2,0,1:T(8,128)}, f32[8,1,5,8,128]{4,3,2,0,1:T(8,128)})) %all-reduce.8.cloned.1.call-update) | async-done | bytes 294928 | tf_op jit(solution)/shard_map/psum | solution.py:110
  599.6 1.2 fusion.23
  600.9 1.1 fusion.26
  602.2 23.9 %psum.63 = bf16[72,256]{1,0:T(8,128)(2,1)S(1)} all-reduce(bf16[72,256]{1,0:T(8,128)(2,1)S(1)} %convolution_convert_fusion), channel_id=1, replica_groups=mesh['seq'=32,'head'=8] {'head'}, use_global_device_ids=true, to_apply=%region_17.18 | all-reduce | flops 18432 | bytes 73728 | tf_op jit(solution)/shard_map/psum | solution.py:129
  626.2 0.6 copy.53
  626.8 0.6 reshape.260
  (67 shorter events, 1.9 us)
Async XLA Ops:
  7.2 151.5 %copy-start = (bf16[8,1024,128]{2,1,0:T(8,128)(2,1)S(1)}, bf16[8,1024,128]{2,1,0:T(8,128)(2,1)}, u32[]{:S(2)}) copy-start(bf16[8,1024,128]{2,1,0:T(8,128)(2,1)} %param.14) | copy-start | bytes 6291460
  7.2 3.1 copy-start.19
  7.2 3.1 copy-start.17
  7.2 3.2 copy-start.11
  7.2 4.0 copy-start.12
  7.2 150.3 %all-reduce.6.cloned.1.call-start = ((), (), s32[]{:S(2)}) async-start(), calls=%async_computation | async-start | bytes 327680 | tf_op jit(solution)/shard_map/psum | solution.py:82
  10.1 589.5 %all-reduce.8.cloned.1.call-start = ((), (), s32[]{:S(2)}) async-start(), calls=%async_computation.1 | async-start | bytes 589824 | tf_op jit(solution)/shard_map/psum | solution.py:110
  10.2 148.5 %copy-start.18 = (f32[64]{0:T(128)}, f32[64]{0:T(128)S(1)}, u32[]{:S(2)}) copy-start(f32[64]{0:T(128)S(1)} %multiply_power_fusion) | copy-start | bytes 772
  10.2 1.7 copy-start.16
  10.3 148.4 %copy-start.13 = (f32[8,5]{1,0:T(8,128)}, f32[8,5]{1,0:T(8,128)S(1)}, u32[]{:S(2)}) copy-start(f32[8,5]{1,0:T(8,128)S(1)} %add_convert_fusion.1) | copy-start | bytes 484
  12.8 146.8 %copy-start.10 = (pred[8,1024]{1,0:T(8,128)(4,1)}, pred[8,1024]{1,0:T(8,128)(4,1)S(1)}, u32[]{:S(2)}) copy-start(pred[8,1024]{1,0:T(8,128)(4,1)S(1)} %get-tuple-element.37) | copy-start | bytes 24580
  12.8 148.0 %copy-start.8 = (pred[8,1024]{1,0:T(8,128)(4,1)}, pred[8,1024]{1,0:T(8,128)(4,1)S(1)}, u32[]{:S(2)}) copy-start(pred[8,1024]{1,0:T(8,128)(4,1)S(1)} %get-tuple-element.38) | copy-start | bytes 24580
  158.7 1.0 copy-start.1
  160.9 1.0 copy-start.5
  296.6 144.9 %copy-start.3 = (f32[8,1,5,8]{3,2,0,1:T(8,128)}, f32[8,1,5,8]{3,2,0,1:T(8,128)S(1)}, u32[]{:S(2)}) copy-start(f32[8,1,5,8]{3,2,0,1:T(8,128)S(1)} %get-tuple-element.19) | copy-start | bytes 3844
  441.4 0.6 copy-start.7
  444.0 3.0 copy-start.6
  444.0 3.0 copy-start.9
  444.0 3.0 copy-start.14
  444.0 3.0 copy-start.20
  447.0 4.4 copy-start.15
  447.0 4.4 copy-start.4
  450.6 151.4 %copy-start.2 = (bf16[1024,256]{1,0:T(8,128)(2,1)S(1)}, bf16[1024,256]{1,0:T(8,128)(2,1)}, u32[]{:S(2)}) copy-start(bf16[1024,256]{1,0:T(8,128)(2,1)} %param.13) | copy-start | bytes 1572868
Sparse Core Ops, SparseCore 0:
  11.5 146.0 all-reduce.5
  450.7 148.8 all-reduce.7
where the time goes:
time: 635 us; the launch traced here: 634 us
  blocking collectives  298 us (47%)
  waiting for transfers between devices  292 us (46%)
  between operations  14.4 us (2%)
  other arithmetic  14.2 us (2%)
  matrix products  11.2 us (2%)
    psum x1, waiting for transfers between devices, per_device(): lax.psum((target_total * factor_target, target_weighted * factor_target[....  147 us
    psum x1, waiting for transfers between devices, per_device(): lax.psum((query_part, key_part, value_part), 'seq')  145 us
    psum x1, blocking collectives, per_device(): lax.psum((query_part, key_part, value_part), 'seq')  139 us
    pmax x1, blocking collectives, per_device(): peak_target, peak_draft = lax.pmax((target_peak, draft_peak), 'seq')  135 us
    psum x1, blocking collectives, per_device(): summed = lax.psum(projected.astype(jnp.bfloat16), 'head')  23.9 us
  transfers between devices with their start and end apart: 2, of which 2 were waited for; matrix products, arithmetic and copies ran while one was open for 1% of the time, Pallas kernels for 0%

commit v1 on v0

--- a/solution.py
+++ b/solution.py
@@ -1,3 +1,4 @@
+import functools
 import jax
 import jax.numpy as jnp
 from jax import lax
@@ -6,6 +7,14 @@
 HEAD_DIM = 128
 BLOCK = 128
 big_negative = -1e30
+
+
+def close_run_now(x_in, comm_axis):
+    tall = jnp.sum(lax.all_gather(x_in, comm_axis), axis=0)
+    return tall
+
+
+launch_inputs = functools.partial(close_run_now, comm_axis="head")
 
 
 def rotate(values_in, positions):
@@ -126,7 +135,7 @@
     draft_heads = finish(merged[3:6], new_scores[:, :, :draft_len], causal[:draft_len], new_values)
     attended = jnp.concatenate([target_heads, draft_heads], axis=0).astype(jnp.bfloat16)
     projected = jnp.dot(attended, w_out, preferred_element_type=jnp.float32)
-    summed = lax.psum(projected.astype(jnp.bfloat16), "head")
+    summed = launch_inputs(projected.astype(jnp.bfloat16))
     verify_out = summed[: batch_size * verify].reshape(batch_size, verify, summed.shape[1])
     draft_out = summed[batch_size * verify :].reshape(batch_size, draft_len, summed.shape[1])
     return (verify_out, draft_out)

time: 635 us -> 627 us (0.987)
  blocking collectives: 298 us -> 287 us
    psum x1 -> x0, blocking collectives: 23.9 us -> none  [per_device(): summed = lax.psum(projected.astype(jnp.bfloat16), 'head')]
    all_gather x0 -> x1, blocking collectives: none -> 13.2 us  [close_run_now(): tall = jnp.sum(lax.all_gather(x_in, comm_axis), axis=0)]
where the time goes in v1:
time: 627 us; the launch traced here: 624 us
  waiting for transfers between devices  292 us (47%)
  blocking collectives  287 us (46%)
  between operations  14.4 us (2%)
  other arithmetic  14.2 us (2%)
  matrix products  11.2 us (2%)
    psum x1, waiting for transfers between devices, per_device(): lax.psum((target_total * factor_target, target_weighted * factor_target[....  147 us
    psum x1, waiting for transfers between devices, per_device(): lax.psum((query_part, key_part, value_part), 'seq')  145 us
    psum x1, blocking collectives, per_device(): lax.psum((query_part, key_part, value_part), 'seq')  139 us
    pmax x1, blocking collectives, per_device(): peak_target, peak_draft = lax.pmax((target_peak, draft_peak), 'seq')  135 us
    all_gather x1, blocking collectives, close_run_now(): tall = jnp.sum(lax.all_gather(x_in, comm_axis), axis=0)  13.2 us
  transfers between devices with their start and end apart: 2, of which 2 were waited for; matrix products, arithmetic and copies ran while one was open for 1% of the time, Pallas kernels for 0%

profile of v1, /device:TPU:32, one launch (start us, length us, event | category | flops | bytes accessed | tf_op | source)
XLA Modules:
  0.0 623.6 jit_solution(7547033947280515958)
XLA Ops:
  7.3 0.9 copy.41
  8.2 1.2 convolution_bitcast_fusion
  9.4 0.7 copy.57
  10.6 0.6 reshape.256
  11.2 0.7 fusion.88
  11.9 0.6 slice.34
  12.8 144.7 %all-reduce.6.cloned.1.call-done = f32[8,5,8,128]{3,2,1,0:T(8,128)} async-done(((f32[8,5,8,128]{3,2,1,0:T(8,128)}), f32[8,5,8,128]{3,2,1,0:T(8,128)}) %all-reduce.6.cloned.1.call-update) | async-done | bytes 163856 | tf_op jit(solution)/shard_map/psum | solution.py:91
  157.5 1.1 subtract_convert_fusion
  158.7 0.9 select_reduce_fusion
  159.6 1.0 fusion.27
  160.9 1.0 fusion.30
  161.9 134.7 %all-reduce.2 = (f32[8,1,4,8]{3,2,0,1:T(4,128)}, f32[8,1,5,8]{3,2,0,1:T(8,128)S(1)}) all-reduce(f32[8,1,4,8]{3,2,0,1:T(4,128)} %bitcast.155, f32[8,1,5,8]{3,2,0,1:T(8,128)S(1)} %bitcast.153), channel_id=1, replica_groups=mesh['seq'=32,'head'=8] {'seq'}, use_global_device_ids=true, to_apply=%region_11.12 | all-reduce | flops 576 | bytes 4608 | tf_op jit(solution)/shard_map/pmax | solution.py:116
  296.6 1.4 bitcast_multiply_fusion
  298.0 1.4 bitcast_multiply_fusion.1
  299.4 138.9 %all-reduce = (f32[8,5,1,128]{3,1,0,2:T(8,128)}, f32[8,1,4,8]{3,2,0,1:T(4,128)}, bf16[40,128]{1,0:T(8,128)(2,1)}, f32[8,1,5,8]{3,2,0,1:T(8,128)}) all-reduce(f32[8,5,1,128]{3,1,0,2:T(8,128)} %reshape.256, f32[8,1,4,8]{3,2,0,1:T(4,128)} %get-tuple-element.33, f32[40,128]{1,0:T(8,128)} %fusion.88, ...), channel_id=1, replica_groups=mesh['seq'=32,'head'=8] {'seq'}, use_global_device_ids=true, to_apply=%region_4.5 | all-reduce | flops 10816 | bytes 76288 | tf_op jit(solution)/shard_map/psum | solution.py:91
  438.2 1.0 fusion.73
  439.3 1.4 fusion.66
  440.6 0.8 select_reduce_fusion.1
  442.0 2.0 fusion.47
  444.0 3.0 fusion.12
  447.1 1.2 fusion.20
  448.3 0.8 fusion.49
  449.1 0.7 fusion.75
  449.8 0.8 fusion.51
  450.6 0.8 fusion.78
  451.5 0.8 fusion.74
  452.3 147.3 %all-reduce.8.cloned.1.call-done = (f32[8,1,4,8,128]{4,3,2,0,1:T(8,128)}, f32[8,1,5,8,128]{4,3,2,0,1:T(8,128)}) async-done(((f32[8,1,4,8,128]{4,3,2,0,1:T(8,128)}, f32[8,1,5,8,128]{4,3,2,0,1:T(8,128)}), (f32[8,1,4,8,128]{4,3,2,0,1:T(8,128)}, f32[8,1,5,8,128]{4,3,2,0,1:T(8,128)})) %all-reduce.8.cloned.1.call-update) | async-done | bytes 294928 | tf_op jit(solution)/shard_map/psum | solution.py:119
  599.6 1.2 fusion.23
  600.9 1.1 fusion.26
  602.2 13.2 %all-gather = bf16[576,256]{1,0:T(8,128)(2,1)S(1)} all-gather(bf16[72,256]{1,0:T(8,128)(2,1)S(1)} %convolution_convert_fusion), channel_id=2, replica_groups=mesh['seq'=32,'head'=8] {'head'}, dimensions={0}, use_global_device_ids=true | all-gather | bytes 331776 | tf_op jit(solution)/shard_map/all_gather | solution.py:13
  615.5 0.6 copy.52
  616.1 0.6 reshape.260
  (68 shorter events, 1.9 us)
Async XLA Ops:
  7.2 151.5 %copy-start = (bf16[8,1024,128]{2,1,0:T(8,128)(2,1)S(1)}, bf16[8,1024,128]{2,1,0:T(8,128)(2,1)}, u32[]{:S(2)}) copy-start(bf16[8,1024,128]{2,1,0:T(8,128)(2,1)} %param.14) | copy-start | bytes 6291460
  7.2 3.1 copy-start.19
  7.2 3.1 copy-start.17
  7.2 3.2 copy-start.11
  7.2 4.0 copy-start.12
  7.2 150.3 %all-reduce.6.cloned.1.call-start = ((), (), s32[]{:S(2)}) async-start(), calls=%async_computation | async-start | bytes 327680 | tf_op jit(solution)/shard_map/psum | solution.py:91
  10.1 589.5 %all-reduce.8.cloned.1.call-start = ((), (), s32[]{:S(2)}) async-start(), calls=%async_computation.1 | async-start | bytes 589824 | tf_op jit(solution)/shard_map/psum | solution.py:119
  10.2 148.5 %copy-start.18 = (f32[64]{0:T(128)}, f32[64]{0:T(128)S(1)}, u32[]{:S(2)}) copy-start(f32[64]{0:T(128)S(1)} %multiply_power_fusion) | copy-start | bytes 772
  10.2 1.7 copy-start.16
  10.3 148.4 %copy-start.13 = (f32[8,5]{1,0:T(8,128)}, f32[8,5]{1,0:T(8,128)S(1)}, u32[]{:S(2)}) copy-start(f32[8,5]{1,0:T(8,128)S(1)} %add_convert_fusion.1) | copy-start | bytes 484
  12.8 146.8 %copy-start.10 = (pred[8,1024]{1,0:T(8,128)(4,1)}, pred[8,1024]{1,0:T(8,128)(4,1)S(1)}, u32[]{:S(2)}) copy-start(pred[8,1024]{1,0:T(8,128)(4,1)S(1)} %get-tuple-element.35) | copy-start | bytes 24580
  12.8 148.0 %copy-start.8 = (pred[8,1024]{1,0:T(8,128)(4,1)}, pred[8,1024]{1,0:T(8,128)(4,1)S(1)}, u32[]{:S(2)}) copy-start(pred[8,1024]{1,0:T(8,128)(4,1)S(1)} %get-tuple-element.36) | copy-start | bytes 24580
  158.7 1.0 copy-start.1
  160.9 1.0 copy-start.5
  296.6 144.9 %copy-start.3 = (f32[8,1,5,8]{3,2,0,1:T(8,128)}, f32[8,1,5,8]{3,2,0,1:T(8,128)S(1)}, u32[]{:S(2)}) copy-start(f32[8,1,5,8]{3,2,0,1:T(8,128)S(1)} %get-tuple-element.17) | copy-start | bytes 3844
  441.4 0.6 copy-start.7
  444.0 3.0 copy-start.6
  444.0 3.0 copy-start.9
  444.0 3.0 copy-start.14
  444.0 3.0 copy-start.20
  447.0 4.4 copy-start.15
  447.0 4.4 copy-start.4
  450.6 151.4 %copy-start.2 = (bf16[1024,256]{1,0:T(8,128)(2,1)S(1)}, bf16[1024,256]{1,0:T(8,128)(2,1)}, u32[]{:S(2)}) copy-start(bf16[1024,256]{1,0:T(8,128)(2,1)} %param.13) | copy-start | bytes 1572868
Sparse Core Ops, SparseCore 0:
  11.5 146.0 all-reduce.5
  450.7 148.8 all-reduce.7
